TPU v7x, 256 devices: a whole 4x4x8 slice. The times are simulated.
256 devices in a mesh: ang: 64 (over x, z, core), sy: 2 (over y_hi), sx: 2 (over y_lo).
Axes of the slice: x: 4, y: 4 (y_hi: 2, y_lo: 2; y = y_hi * 2 + y_lo), z: 8, core: 2. Of those that a mesh axis runs over, the one named last changes fastest.
Arguments:
- objects: bfloat16 [64, 2, 1024, 1024], P('ang', None, 'sy', 'sx'), may hold values from -4 to 4
- probe: float32 [2, 2, 256, 256], replicated, may hold values from -4 to 4
- data: bfloat16 [64, 2, 2, 2, 256, 256], P('ang', 'sy', 'sx'), may hold values from 0 to 4
- positions: int32 [64, 2, 2, 2, 2], P('ang', 'sy', 'sx'), may hold values from 0 to 384
- block_index: int32 [8, 16], replicated, may hold values from 0 to 511, as said below
- block_values: bfloat16 [8, 16, 128, 128], replicated, may hold values from -0.125 to 0.125
Outputs:
- object_grad: float32 [64, 2, 1024, 1024], P('ang', None, 'sy', 'sx')
- probe_grad: float32 [64, 2, 2, 256, 256], P('ang')
- vol_grad: float32 [2, 512, 2, 1024], P('sy', ('ang', 'sx'))
Inputs may be any that keep to these rules, and one draw needn't show every extreme that they name: `positions`: A position counts cells from 64 cells before the tile's first row or column. `block_index`: entry g names the angle g // 8 and the column block g % 8; every angle is named by exactly 2 entries.
All inputs are finite; a program needn't handle non-finite values.
Results may differ from a plain program's by a relative error of at most 0.011.
Values may be sent and summed in bfloat16 or wider, within the bound.
A program may use at most 64 MiB of HBM per device.

v0:
```python
from functools import partial
import math
import jax
import jax.numpy as jnp
from jax import lax
from jax.sharding import PartitionSpec as P

PATCH = 256
RIM = 64
BLK = 128


def with_halo(cells, sides, width):
    for axis, dim in sides:
        count = lax.axis_size(axis)
        ends = count - 1
        head = lax.slice_in_dim(cells, 0, width, axis=dim)
        tail = lax.slice_in_dim(cells, cells.shape[dim] - width, cells.shape[dim], axis=dim)
        cells = jnp.concatenate(
            [
                lax.ppermute(tail, axis, [(i, (i + 1) % count) for i in range(ends)]),
                cells,
                lax.ppermute(head, axis, [((i + 1) % count, i) for i in range(ends)]),
            ],
            axis=dim,
        )
    return cells


def dft_parts(length):
    sample_ids = jnp.arange(length, dtype=jnp.int32)
    product = sample_ids[:, None] * sample_ids[None, :] % length
    phases = product.astype(jnp.float32) * (2.0 * math.pi / length)
    factor = 1.0 / math.sqrt(length)
    return (jnp.cos(phases) * factor, -jnp.sin(phases) * factor)


def dft_blocks(length):
    real_part, imag_part = dft_parts(length)
    forward = jnp.stack(
        [jnp.stack([real_part, -imag_part], 1), jnp.stack([imag_part, real_part], 1)], 0
    )
    backward = jnp.stack(
        [jnp.stack([real_part, imag_part], 1), jnp.stack([-imag_part, real_part], 1)], 0
    )
    return (forward.astype(jnp.bfloat16), backward.astype(jnp.bfloat16))


def ramp_table(width):
    column_ids = jnp.arange(width, dtype=jnp.int32)
    offsets = column_ids[None, :] - column_ids[:, None]
    odd_cells = offsets % 2 != 0
    scaled = offsets.astype(jnp.float32) * math.pi
    values = jnp.where(odd_cells, -1.0 / jnp.maximum(scaled * scaled, 1.0), 0.0)
    values = jnp.where(offsets == 0, 0.25, values)
    return values.astype(jnp.bfloat16)


def left_product(matrix, fields):
    return jnp.einsum("srtk,btkc->bsrc", matrix, fields, preferred_element_type=jnp.float32)


def right_product(fields, matrix):
    return jnp.einsum("btrc,tcsq->bsrq", fields, matrix, preferred_element_type=jnp.float32)


def cut_window(field, corner):
    return lax.dynamic_slice(
        field, (jnp.int32(0), corner[0], corner[1]), (field.shape[0], PATCH, PATCH)
    )


def patch_gradients(patches, measured, probe, forward, backward):
    patch_count = patches.shape[0]
    mode_count = probe.shape[0]
    side = patches.shape[2]
    object_real = patches[:, 0].astype(jnp.float32)[:, None]
    object_imag = patches[:, 1].astype(jnp.float32)[:, None]
    probe_real = probe[None, :, 0]
    probe_imag = probe[None, :, 1]
    exit_real = probe_real * object_real - probe_imag * object_imag
    exit_imag = probe_real * object_imag + probe_imag * object_real
    exit_waves = (
        jnp.stack([exit_real, exit_imag], 2)
        .reshape(patch_count * mode_count, 2, side, side)
        .astype(jnp.bfloat16)
    )
    half_done = left_product(forward, exit_waves).astype(jnp.bfloat16)
    far_field = right_product(half_done, backward).reshape(patch_count, mode_count, 2, side, side)
    intensity = jnp.sum(far_field * far_field, axis=(1, 2))
    misfit = intensity - measured.astype(jnp.float32)
    weighted = (
        (misfit[:, None, None] * far_field)
        .reshape(patch_count * mode_count, 2, side, side)
        .astype(jnp.bfloat16)
    )
    back_half = left_product(backward, weighted).astype(jnp.bfloat16)
    spread = right_product(back_half, forward).reshape(patch_count, mode_count, 2, side, side)
    chi_real = spread[:, :, 0]
    chi_imag = spread[:, :, 1]
    grad_real = jnp.sum(probe_real * chi_real + probe_imag * chi_imag, axis=1)
    grad_imag = jnp.sum(probe_real * chi_imag - probe_imag * chi_real, axis=1)
    patch_grad = jnp.stack([grad_real, grad_imag], 1)
    probe_real_part = jnp.sum(object_real * chi_real + object_imag * chi_imag, axis=0)
    probe_imag_part = jnp.sum(object_real * chi_imag - object_imag * chi_real, axis=0)
    probe_part = jnp.stack([probe_real_part, probe_imag_part], 1)
    return (patch_grad, probe_part)


def fold_rims(field, axis_at, extent):
    inside = lax.slice_in_dim(field, 2 * RIM, 2 * RIM + extent, axis=axis_at)
    leading = lax.slice_in_dim(field, 0, RIM, axis=axis_at)
    trailing = lax.slice_in_dim(field, extent + 3 * RIM, extent + 4 * RIM, axis=axis_at)
    widths_lead = [(0, 0)] * field.ndim
    widths_lead[axis_at] = (0, extent - RIM)
    widths_trail = [(0, 0)] * field.ndim
    widths_trail[axis_at] = (extent - RIM, 0)
    return inside + jnp.pad(leading, widths_lead) + jnp.pad(trailing, widths_trail)


def body(objects, probe, data, positions, block_index, block_values):
    forward, backward = dft_blocks(PATCH)
    tile_rows = objects.shape[2]
    tile_cols = objects.shape[3]
    padded = with_halo(objects[0], (("sy", 1), ("sx", 2)), RIM)
    starts = positions[0, 0, 0]
    patches = jax.vmap(partial(cut_window, padded))(starts)
    patch_grad, probe_part = patch_gradients(patches, data[0, 0, 0], probe, forward, backward)

    def place_patch(grad_piece, corner):
        empty = jnp.zeros(padded.shape, jnp.float32)
        return lax.dynamic_update_slice(empty, grad_piece, (jnp.int32(0), corner[0], corner[1]))

    running_sum = jnp.sum(jax.vmap(place_patch)(patch_grad, starts), axis=0)
    returned = with_halo(running_sum.astype(jnp.bfloat16), (("sy", 1), ("sx", 2)), RIM).astype(
        running_sum.dtype
    )
    object_grad = fold_rims(fold_rims(returned, 1, tile_rows), 2, tile_cols)
    tile_count = lax.axis_size("sy") * lax.axis_size("sx")
    probe_total = lax.psum(probe_part.astype(jnp.bfloat16), ("sy", "sx")).astype(jnp.float32)
    probe_grad = (probe_total / math.sqrt(starts.shape[0] * tile_count))[None]
    line_blocks = block_values.shape[0]
    width_all = line_blocks * block_values.shape[2]
    angle_count = lax.axis_size("ang")
    column_parts = lax.axis_size("sx")
    rows_here = tile_rows // (angle_count * column_parts)
    ramp_matrix = ramp_table(width_all)
    sinogram = object_grad.astype(jnp.bfloat16)[None]
    ramp_split = ramp_matrix.reshape(column_parts, tile_cols, width_all)
    received = lax.all_to_all(sinogram, ("ang", "sx"), split_axis=2, concat_axis=0, tiled=True)
    shaped = received.reshape(angle_count, column_parts, received.shape[1], rows_here, tile_cols)
    result = jnp.einsum("ascrt,stv->acrv", shaped, ramp_split, preferred_element_type=jnp.float32)
    filtered = result.astype(jnp.bfloat16)
    line_data = filtered.reshape(filtered.shape[0], 2, rows_here, line_blocks, BLK)
    angle_of = block_index // line_blocks
    column_of = block_index % line_blocks
    picked = line_data[angle_of, :, :, column_of, :]
    volume = jnp.einsum(
        "bkcru,bkuv->rcbv", picked, block_values, preferred_element_type=jnp.float32
    )
    vol_grad = volume.reshape(1, rows_here, 2, width_all)
    return (object_grad[None], probe_grad, vol_grad)


def solution(mesh):
    placed = (
        P("ang", None, "sy", "sx"),
        P(),
        P("ang", "sy", "sx", None, None, None),
        P("ang", "sy", "sx", None, None),
        P(),
        P(),
    )
    return jax.shard_map(
        body,
        mesh=mesh,
        in_specs=placed,
        out_specs=(
            P("ang", None, "sy", "sx"),
            P("ang", None, None, None, None),
            P("sy", ("ang", "sx"), None, None),
        ),
        check_vma=False,
    )
```

profile of v0, /device:TPU:2, one launch (start us, length us, event | category | flops | bytes accessed | tf_op | source)
XLA Modules:
  0.0 221.8 jit_solution(13552120313437192784)
XLA Ops:
  7.2 1.1 fusion.79
  8.3 5.1 %collective-permute-start = (bf16[2,64,512]{2,1,0:T(8,128)(2,1)S(1)}, bf16[2,64,512]{2,1,0:T(8,128)(2,1)S(1)}, u32[]{:S(2)}, u32[]{:S(2)}) collective-permute-start(bf16[2,64,512]{2,1,0:T(8,128)(2,1)S(1)} %get-tuple-element.75), channel_id=1, source_target_pairs={{0,2},{1,3},{4,6},{5,7},{8,10},{9,11},{12,14},{13,15},{16,18},{17,... | collective-permute-start | bytes 393224 | tf_op jit(solution)/shard_map/ppermute | solution.py:21
  13.4 1.3 collective-permute-start.1
  14.7 1.0 fusion.55
  15.7 1.0 multiply_convert_fusion
  16.7 1.0 negate_convert_fusion
  17.6 0.8 compare_select_fusion.3
  18.5 1.3 slice_bitcast_fusion.3
  19.8 0.7 broadcast_clamp_fusion
  20.5 0.8 fusion.47
  21.3 0.4 collective-permute-done.1
  22.0 1.0 pad_maximum_fusion.8
  23.0 3.3 %collective-permute-start.2 = (bf16[2,640,64]{2,1,0:T(8,128)(2,1)}, bf16[2,640,64]{2,1,0:T(8,128)(2,1)}, u32[]{:S(2)}, u32[]{:S(2)}) collective-permute-start(bf16[2,640,64]{2,1,0:T(8,128)(2,1)} %get-tuple-element.71), channel_id=1, source_target_pairs={{0,1},{2,3},{4,5},{6,7},{8,9},{10,11},{12,13},{14,15},{16,17},{18,... | collective-permute-start | bytes 491528 | tf_op jit(solution)/shard_map/ppermute | solution.py:21
  26.3 1.5 collective-permute-start.3
  28.0 1.0 copy.50
  29.0 1.8 copy.54
  30.8 2.0 maximum_bitcast_fusion.3
  32.9 4.5 %collective-permute-done.3 = bf16[2,640,64]{2,1,0:T(8,128)(2,1)} collective-permute-done((bf16[2,640,64]{2,1,0:T(8,128)(2,1)}, bf16[2,640,64]{2,1,0:T(8,128)(2,1)}, u32[]{:S(2)}, u32[]{:S(2)}) %collective-permute-start.3) | collective-permute-done | bytes 163872 | tf_op jit(solution)/shard_map/ppermute | solution.py:23
  37.4 2.2 pad_maximum_fusion
  39.6 5.8 %while.2 = (s32[]{:T(128)}, bf16[2,640,640]{2,1,0:T(8,128)(2,1)S(1)}, s32[2,3]{1,0:T(2,128)S(1)}, bf16[2,2,256,256]{3,2,1,0:T(8,128)(2,1)}, s32[]{:T(128)}) while((s32[]{:T(128)}, bf16[2,640,640]{2,1,0:T(8,128)(2,1)S(1)}, s32[2,3]{1,0:T(2,128)S(1)}, bf16[2,2,256,256]{3,2,1,0:T(8,128)(2,1)}, s32[]{:T(128)}) %tuple.63), condition=%wide.while_cond, body=%wide.while_body.sunk | while | flops 2 | bytes 525929 | solution.py:68
  39.6 0.7 fusion.86
  40.2 2.2 %bitcast_dynamic-update-slice_fusion.2 = bf16[2,2,256,256]{3,2,1,0:T(8,128)(2,1)} fusion(bf16[2,2,256,256]{3,2,1,0:T(8,128)(2,1)} %get-tuple-element.161, s32[]{:T(128)} %get-tuple-element.158, bf16[2,640,640]{2,1,0:T(8,128)(2,1)S(1)} %get-tuple-element.164, s32[]{:T(128)} %bitcast.203, s32[]{:T(128)} %bitcast.204), kind=kLoop, calls=%fused_computation.1.clone.1 | loop fusion | bytes 525824 | tf_op jit(solution)/shard_map/vmap()/gather
  42.5 0.7 fusion.86
  43.1 2.2 %bitcast_dynamic-update-slice_fusion.2 = bf16[2,2,256,256]{3,2,1,0:T(8,128)(2,1)} fusion(bf16[2,2,256,256]{3,2,1,0:T(8,128)(2,1)} %get-tuple-element.161, s32[]{:T(128)} %get-tuple-element.158, bf16[2,640,640]{2,1,0:T(8,128)(2,1)S(1)} %get-tuple-element.164, s32[]{:T(128)} %bitcast.203, s32[]{:T(128)} %bitcast.204), kind=kLoop, calls=%fused_computation.1.clone.1 | loop fusion | bytes 525824 | tf_op jit(solution)/shard_map/vmap()/gather
  45.4 1.2 bitcast_convert_fusion.4
  47.0 1.3 subtract_convert_fusion
  48.3 5.0 %fusion.15 = (f32[4,256,256]{1,2,0:T(8,128)}, f32[2,256,4,256,1]{3,1,4,2,0:T(8,128)}) fusion(bf16[4,1,256,256]{2,3,1,0:T(8,128)(2,1)} %bitcast.227, bf16[4,1,256,256]{2,3,1,0:T(8,128)(2,1)} %bitcast.226, bf16[1,256,2,256]{3,1,2,0:T(8,128)(2,1)S(1)} %copy-done.10, bf16[1,256,2,256]{3,1,2,0:T(8,128)(2,1)S(1)} %copy-done.9, ...), kind=kOutput, calls=%fused_computation.31 | convolution fusion | flops 1078198272 | bytes 5242880 | tf_op jit(solution)/shard_map/btrc,tcsq->bsrq/dot_general | solution.py:64
  53.3 1.4 bitcast_reduce_fusion
  54.7 1.1 mul.359
  55.8 3.4 %fusion.33 = f32[2,256,4,256,1]{3,1,4,2,0:T(8,128)S(1)} fusion(bf16[2,256,2,256,1]{3,1,2,0,4:T(8,128)(2,1)} %get-tuple-element.89, bf16[1,256,2,256]{3,1,2,0:T(8,128)(2,1)S(1)} %get-tuple-element.80, bf16[1,256,2,256]{3,1,2,0:T(8,128)(2,1)} %copy-done.5, f32[2,256,4,256,1]{3,1,4,2,0:T(8,128)} %get-tuple-element.88, f32[4,256,256]{1,2,0:T(8,128)} %bitcast.218), kind=kOutput, calls=%fused_computation.49 | convolution fusion | flops 1076363264 | bytes 6291456 | tf_op jit(solution)/shard_map/btrc,tcsq->bsrq/dot_general | solution.py:64
  59.2 2.7 %add_reduce_fusion = (bf16[2,256,256]{1,2,0:T(8,128)(2,1)S(1)}, bf16[2,256,256]{1,2,0:T(8,128)(2,1)}, f32[2,256,256]{1,2,0:T(8,128)S(1)}, f32[2,256,256]{1,2,0:T(8,128)S(1)}) fusion(f32[2,2,2,256,256]{3,4,1,0,2:T(8,128)S(1)} %bitcast.212, f32[2,256,256]{1,2,0:T(8,128)} %copy-done.4, f32[2,256,256]{1,2,0:T(8,128)} %copy-done.3, ...), kind=kLoop, calls=%fused_computation.64 | loop fusion | flops 3670016 | bytes 5767168 | tf_op jit(solution)/shard_map/reduce_sum | solution.py:104
  62.0 3.1 %broadcast_in_dim.40 = f32[2,2,640,640]{3,2,1,0:T(8,128)} broadcast(f32[]{:T(128)} %constant.70.clone.1), dimensions={} | broadcast | bytes 6553604 | tf_op jit(solution)/shard_map/vmap(vmap())/broadcast_in_dim;vmap()/broadcast_in_dim | solution.py:132
  65.1 33.3 %while.3 = (s32[]{:T(128)}, f32[2,2,640,640]{3,2,1,0:T(8,128)}, s32[2,4]{1,0:T(2,128)S(1)}, f32[2,2,256,256]{2,3,0,1:T(8,128)S(1)}, s32[]{:T(128)}, /*index=5*/s32[4]{0:T(128)S(1)}, s32[]{:T(128)}) while((s32[]{:T(128)}, f32[2,2,640,640]{3,2,1,0:T(8,128)}, s32[2,4]{1,0:T(2,128)S(1)}, f32[2,2,256,256]{2,3,0,1:T(8,128)S(1)}, s32[]{:T(128)}, ...), condition=%wide.while_cond.1, body=%wide.while_body.1.sunk | while | flops 131101 | bytes 4718791 | solution.py:132
  65.1 0.7 fusion.87
  65.8 3.3 %and_reduce_fusion.2 = pred[]{:T(512)} fusion(s32[4]{0:T(128)S(1)} %get-tuple-element.187, s32[1]{0:T(128)} %bitcast.208, s32[1]{0:T(128)} %bitcast.209, s32[1]{0:T(128)} %bitcast.210, s32[1]{0:T(128)} %bitcast.211), kind=kLoop, calls=%fused_computation.4.clone.1 | loop fusion | flops 27 | bytes 33 | tf_op jit(solution)/shard_map/vmap(vmap())/scatter
  69.3 3.9 %dynamic-slice_select_fusion.2 = f32[1,2,256,256]{3,2,1,0:T(8,128)S(1)} fusion(f32[1,2,256,256]{3,2,1,0:T(8,128)S(1)} %copy.105, f32[2,2,640,640]{3,2,1,0:T(8,128)} %get-tuple-element.176, s32[]{:T(128)} %bitcast.205, s32[]{:T(128)} %bitcast.206, s32[]{:T(128)} %bitcast.207, pred[]{:T(512)} %and_reduce_fusion.2), kind=kLoop, calls=%fused_computation.3.clone.1 | loop fusion | flops 131072 | bytes 1572877 | tf_op jit(solution)/shard_map/vmap(vmap())/scatter
  73.3 8.4 %dynamic-update-slice.8 = f32[2,2,640,640]{3,2,1,0:T(8,128)} dynamic-update-slice(f32[2,2,640,640]{3,2,1,0:T(8,128)} %get-tuple-element.176, f32[1,2,256,256]{3,2,1,0:T(8,128)S(1)} %dynamic-slice_select_fusion.2, s32[]{:T(128)} %bitcast.205, s32[]{:T(128)} %constant.71.clone.1..sunk, s32[]{:T(128)} %bitcast.206, s32[]{:T(128)} %bitcast.207) | dynamic-update-slice | bytes 1048580 | tf_op jit(solution)/shard_map/vmap(vmap())/scatter
  81.7 0.7 fusion.87
  82.4 3.3 %and_reduce_fusion.2 = pred[]{:T(512)} fusion(s32[4]{0:T(128)S(1)} %get-tuple-element.187, s32[1]{0:T(128)} %bitcast.208, s32[1]{0:T(128)} %bitcast.209, s32[1]{0:T(128)} %bitcast.210, s32[1]{0:T(128)} %bitcast.211), kind=kLoop, calls=%fused_computation.4.clone.1 | loop fusion | flops 27 | bytes 33 | tf_op jit(solution)/shard_map/vmap(vmap())/scatter
  85.9 3.9 %dynamic-slice_select_fusion.2 = f32[1,2,256,256]{3,2,1,0:T(8,128)S(1)} fusion(f32[1,2,256,256]{3,2,1,0:T(8,128)S(1)} %copy.105, f32[2,2,640,640]{3,2,1,0:T(8,128)} %get-tuple-element.176, s32[]{:T(128)} %bitcast.205, s32[]{:T(128)} %bitcast.206, s32[]{:T(128)} %bitcast.207, pred[]{:T(512)} %and_reduce_fusion.2), kind=kLoop, calls=%fused_computation.3.clone.1 | loop fusion | flops 131072 | bytes 1572877 | tf_op jit(solution)/shard_map/vmap(vmap())/scatter
  89.8 8.6 %dynamic-update-slice.8 = f32[2,2,640,640]{3,2,1,0:T(8,128)} dynamic-update-slice(f32[2,2,640,640]{3,2,1,0:T(8,128)} %get-tuple-element.176, f32[1,2,256,256]{3,2,1,0:T(8,128)S(1)} %dynamic-slice_select_fusion.2, s32[]{:T(128)} %bitcast.205, s32[]{:T(128)} %constant.71.clone.1..sunk, s32[]{:T(128)} %bitcast.206, s32[]{:T(128)} %bitcast.207) | dynamic-update-slice | bytes 1048580 | tf_op jit(solution)/shard_map/vmap(vmap())/scatter
  98.4 3.8 %reduce_sum.66 = bf16[2,640,640]{2,1,0:T(8,128)(2,1)S(1)} reduce(f32[2,2,640,640]{3,2,1,0:T(8,128)} %get-tuple-element.16, f32[]{:T(128)} %constant.70.clone.1), dimensions={0}, to_apply=%region_5.6 | reduce | flops 819200 | bytes 8192004 | tf_op jit(solution)/shard_map/reduce_sum | solution.py:134
  102.2 5.6 %collective-permute-start.4 = (bf16[2,64,640]{2,1,0:T(8,128)(2,1)S(1)}, bf16[2,64,640]{2,1,0:T(8,128)(2,1)S(1)}, u32[]{:S(2)}, u32[]{:S(2)}) collective-permute-start(bf16[2,64,640]{2,1,0:T(8,128)(2,1)S(1)} %get-tuple-element.69), channel_id=1, source_target_pairs={{0,2},{1,3},{4,6},{5,7},{8,10},{9,11},{12,14},{13,15},{16,18},{17,... | collective-permute-start | bytes 491528 | tf_op jit(solution)/shard_map/ppermute | solution.py:21
  107.9 1.3 collective-permute-start.5
  109.2 1.5 collective-permute-done.4
  110.7 6.3 %collective-permute-done.5 = bf16[2,64,640]{2,1,0:T(8,128)(2,1)S(1)} collective-permute-done((bf16[2,64,640]{2,1,0:T(8,128)(2,1)S(1)}, bf16[2,64,640]{2,1,0:T(8,128)(2,1)S(1)}, u32[]{:S(2)}, u32[]{:S(2)}) %collective-permute-start.5) | collective-permute-done | bytes 163872 | tf_op jit(solution)/shard_map/ppermute | solution.py:23
  117.1 1.3 collective-permute-start.6
  118.5 1.3 collective-permute-start.7
  119.8 4.3 %collective-permute-done.6 = bf16[2,768,64]{2,1,0:T(8,128)(2,1)S(1)} collective-permute-done((bf16[2,768,64]{2,1,0:T(8,128)(2,1)S(1)}, bf16[2,768,64]{2,1,0:T(8,128)(2,1)S(1)}, u32[]{:S(2)}, u32[]{:S(2)}) %collective-permute-start.6) | collective-permute-done | bytes 196640 | tf_op jit(solution)/shard_map/ppermute | solution.py:21
  124.1 4.1 %collective-permute-done.7 = bf16[2,768,64]{2,1,0:T(8,128)(2,1)S(1)} collective-permute-done((bf16[2,768,64]{2,1,0:T(8,128)(2,1)S(1)}, bf16[2,768,64]{2,1,0:T(8,128)(2,1)S(1)}, u32[]{:S(2)}, u32[]{:S(2)}) %collective-permute-start.7) | collective-permute-done | bytes 196640 | tf_op jit(solution)/shard_map/ppermute | solution.py:23
  128.3 2.0 maximum_convert_fusion
  131.0 1.8 convert_bitcast_fusion
  132.7 2.1 copy.59
  134.8 14.4 %all-to-all-start = ((bf16[1,2,512,512]{3,1,0,2:T(2,128)(2,1)}), bf16[1,2,512,512]{3,1,0,2:T(2,128)(2,1)S(1)}, u32[]{:S(2)}, u32[]{:S(2)}) async-start(bf16[1,2,512,512]{3,1,0,2:T(2,128)(2,1)} %copy.59), calls=%async_computation | async-start | bytes 2097152 | tf_op jit(solution)/shard_map/all_to_all | solution.py:150
  149.3 0.8 pad_maximum_fusion.2
  150.3 50.9 %all-reduce.4.cloned.1.call-done = bf16[2,2,256,256]{2,3,0,1:T(8,128)(2,1)} async-done(((bf16[2,2,256,256]{2,3,0,1:T(8,128)(2,1)}), bf16[2,2,256,256]{2,3,0,1:T(8,128)(2,1)}) %all-reduce.4.cloned.1.call-update) | async-done | bytes 524304 | tf_op jit(solution)/shard_map/psum | solution.py:140
  201.2 1.1 multiply_bitcast_fusion
  202.3 1.3 copy.66
  203.6 0.4 copy.60
  204.1 4.6 %bitcast_convert_fusion = bf16[64,2,4,1024]{3,0,2,1:T(8,128)(2,1)S(1)} fusion(s32[2,512]{1,0:T(2,128)S(1)} %multiply_add_fusion, bf16[64,2,2,4,512]{4,3,2,1,0:T(4,128)(2,1)S(1)} %bitcast.222), kind=kOutput, calls=%fused_computation.33 | convolution fusion | flops 1097334784 | bytes 2101248 | tf_op jit(solution)/shard_map/ascrt,stv->acrv/dot_general | solution.py:152
  209.0 1.4 copy.62
  210.3 1.0 gather_fusion
  211.3 2.9 %fusion.30 = f32[4,2,8,128]{3,0,1,2:T(4,128)S(1)} fusion(bf16[8,16,2,4,128]{4,3,2,1,0:T(4,128)(2,1)S(1)} %bitcast.221, bf16[8,16,128,128]{3,2,1,0:T(8,128)(2,1)} %param.11), kind=kOutput, calls=%fused_computation.48 | convolution fusion | flops 33554432 | bytes 4489216 | tf_op jit(solution)/shard_map/bkcru,bkuv->rcbv/dot_general | solution.py:158
  214.3 0.6 reshape.313
  (64 shorter events, 3.0 us)
Async XLA Ops:
  7.2 14.8 %copy-start = (bf16[1,2,512,512]{3,2,1,0:T(8,128)(2,1)S(1)}, bf16[1,2,512,512]{3,2,1,0:T(8,128)(2,1)}, u32[]{:S(2)}) copy-start(bf16[1,2,512,512]{3,2,1,0:T(8,128)(2,1)} %param.6) | copy-start | bytes 3145732
  8.3 13.0 %collective-permute-start = (bf16[2,64,512]{2,1,0:T(8,128)(2,1)S(1)}, bf16[2,64,512]{2,1,0:T(8,128)(2,1)S(1)}, u32[]{:S(2)}, u32[]{:S(2)}) collective-permute-start(bf16[2,64,512]{2,1,0:T(8,128)(2,1)S(1)} %get-tuple-element.75), channel_id=1, source_target_pairs={{0,2},{1,3},{4,6},{5,7},{8,10},{9,11},{12,14},{13,15},{16,18},{17,... | collective-permute-start | bytes 393224 | tf_op jit(solution)/shard_map/ppermute | solution.py:21
  13.4 8.4 %collective-permute-start.1 = (bf16[2,64,512]{2,1,0:T(8,128)(2,1)S(1)}, bf16[2,64,512]{2,1,0:T(8,128)(2,1)S(1)}, u32[]{:S(2)}, u32[]{:S(2)}) collective-permute-start(bf16[2,64,512]{2,1,0:T(8,128)(2,1)S(1)} %get-tuple-element.76), channel_id=1, source_target_pairs={{2,0},{3,1},{6,4},{7,5},{10,8},{11,9},{14,12},{15,13},{18,16},{19,... | collective-permute-start | bytes 393224 | tf_op jit(solution)/shard_map/ppermute | solution.py:23
  21.3 11.6 %copy-start.5 = (bf16[1,256,2,256]{3,1,2,0:T(8,128)(2,1)}, bf16[1,256,2,256]{3,1,2,0:T(8,128)(2,1)S(1)}, u32[]{:S(2)}) copy-start(bf16[1,256,2,256]{3,1,2,0:T(8,128)(2,1)S(1)} %get-tuple-element.83) | copy-start | bytes 786436
  21.3 11.6 %copy-start.8 = (bf16[1,256,2,256]{3,1,2,0:T(8,128)(2,1)}, bf16[1,256,2,256]{3,1,2,0:T(8,128)(2,1)S(1)}, u32[]{:S(2)}) copy-start(bf16[1,256,2,256]{3,1,2,0:T(8,128)(2,1)S(1)} %get-tuple-element.79) | copy-start | bytes 786436
  21.3 0.7 copy-start.11
  22.0 1.0 copy-start.12
  23.0 9.9 %collective-permute-start.2 = (bf16[2,640,64]{2,1,0:T(8,128)(2,1)}, bf16[2,640,64]{2,1,0:T(8,128)(2,1)}, u32[]{:S(2)}, u32[]{:S(2)}) collective-permute-start(bf16[2,640,64]{2,1,0:T(8,128)(2,1)} %get-tuple-element.71), channel_id=1, source_target_pairs={{0,1},{2,3},{4,5},{6,7},{8,9},{10,11},{12,13},{14,15},{16,17},{18,... | collective-permute-start | bytes 491528 | tf_op jit(solution)/shard_map/ppermute | solution.py:21
  26.3 11.1 %collective-permute-start.3 = (bf16[2,640,64]{2,1,0:T(8,128)(2,1)}, bf16[2,640,64]{2,1,0:T(8,128)(2,1)}, u32[]{:S(2)}, u32[]{:S(2)}) collective-permute-start(bf16[2,640,64]{2,1,0:T(8,128)(2,1)} %get-tuple-element.72), channel_id=1, source_target_pairs={{1,0},{3,2},{5,4},{7,6},{9,8},{11,10},{13,12},{15,14},{17,16},{19,... | collective-permute-start | bytes 491528 | tf_op jit(solution)/shard_map/ppermute | solution.py:23
  39.5 7.4 %copy-start.1 = (f32[2,256,256]{1,2,0:T(8,128)S(1)}, f32[2,256,256]{1,2,0:T(8,128)}, u32[]{:S(2)}) copy-start(f32[2,256,256]{1,2,0:T(8,128)} %copy.50) | copy-start | bytes 1572868
  45.4 2.9 %copy-start.9 = (bf16[1,256,2,256]{3,1,2,0:T(8,128)(2,1)S(1)}, bf16[1,256,2,256]{3,1,2,0:T(8,128)(2,1)}, u32[]{:S(2)}) copy-start(bf16[1,256,2,256]{3,1,2,0:T(8,128)(2,1)} %copy-done.8) | copy-start | bytes 786436
  45.4 2.9 %copy-start.10 = (bf16[1,256,2,256]{3,1,2,0:T(8,128)(2,1)S(1)}, bf16[1,256,2,256]{3,1,2,0:T(8,128)(2,1)}, u32[]{:S(2)}) copy-start(bf16[1,256,2,256]{3,1,2,0:T(8,128)(2,1)} %get-tuple-element.84) | copy-start | bytes 786436
  46.8 6.5 %copy-start.3 = (f32[2,256,256]{1,2,0:T(8,128)}, f32[2,256,256]{1,2,0:T(8,128)S(1)}, u32[]{:S(2)}) copy-start(f32[2,256,256]{1,2,0:T(8,128)S(1)} %copy.49) | copy-start | bytes 1572868
  47.0 6.3 %copy-start.4 = (f32[2,256,256]{1,2,0:T(8,128)}, f32[2,256,256]{1,2,0:T(8,128)S(1)}, u32[]{:S(2)}) copy-start(f32[2,256,256]{1,2,0:T(8,128)S(1)} %copy.51) | copy-start | bytes 1572868
  48.3 6.4 %copy-start.6 = (bf16[1,1,1,2,256,256]{4,5,3,2,1,0:T(8,128)(2,1)S(1)}, bf16[1,1,1,2,256,256]{4,5,3,2,1,0:T(8,128)(2,1)}, u32[]{:S(2)}) copy-start(bf16[1,1,1,2,256,256]{4,5,3,2,1,0:T(8,128)(2,1)} %copy.54) | copy-start | bytes 786436
  55.8 3.4 %copy-start.2 = (f32[2,256,256]{1,2,0:T(8,128)S(1)}, f32[2,256,256]{1,2,0:T(8,128)}, u32[]{:S(2)}) copy-start(f32[2,256,256]{1,2,0:T(8,128)} %copy.50) | copy-start | bytes 1572868
  62.0 3.2 %copy-start.13 = (s32[4]{0:T(128)S(1)}, s32[4]{0:T(128)}, u32[]{:S(2)}) copy-start(s32[4]{0:T(128)} %constant.300) | copy-start | bytes 52
  102.2 8.4 %collective-permute-start.4 = (bf16[2,64,640]{2,1,0:T(8,128)(2,1)S(1)}, bf16[2,64,640]{2,1,0:T(8,128)(2,1)S(1)}, u32[]{:S(2)}, u32[]{:S(2)}) collective-permute-start(bf16[2,64,640]{2,1,0:T(8,128)(2,1)S(1)} %get-tuple-element.69), channel_id=1, source_target_pairs={{0,2},{1,3},{4,6},{5,7},{8,10},{9,11},{12,14},{13,15},{16,18},{17,... | collective-permute-start | bytes 491528 | tf_op jit(solution)/shard_map/ppermute | solution.py:21
  107.9 9.1 %collective-permute-start.5 = (bf16[2,64,640]{2,1,0:T(8,128)(2,1)S(1)}, bf16[2,64,640]{2,1,0:T(8,128)(2,1)S(1)}, u32[]{:S(2)}, u32[]{:S(2)}) collective-permute-start(bf16[2,64,640]{2,1,0:T(8,128)(2,1)S(1)} %get-tuple-element.70), channel_id=1, source_target_pairs={{2,0},{3,1},{6,4},{7,5},{10,8},{11,9},{14,12},{15,13},{18,16},{19,... | collective-permute-start | bytes 491528 | tf_op jit(solution)/shard_map/ppermute | solution.py:23
  117.1 6.9 %collective-permute-start.6 = (bf16[2,768,64]{2,1,0:T(8,128)(2,1)S(1)}, bf16[2,768,64]{2,1,0:T(8,128)(2,1)S(1)}, u32[]{:S(2)}, u32[]{:S(2)}) collective-permute-start(bf16[2,768,64]{2,1,0:T(8,128)(2,1)S(1)} %get-tuple-element.67), channel_id=1, source_target_pairs={{0,1},{2,3},{4,5},{6,7},{8,9},{10,11},{12,13},{14,15},{16,17},{18,... | collective-permute-start | bytes 589832 | tf_op jit(solution)/shard_map/ppermute | solution.py:21
  118.5 9.7 %collective-permute-start.7 = (bf16[2,768,64]{2,1,0:T(8,128)(2,1)S(1)}, bf16[2,768,64]{2,1,0:T(8,128)(2,1)S(1)}, u32[]{:S(2)}, u32[]{:S(2)}) collective-permute-start(bf16[2,768,64]{2,1,0:T(8,128)(2,1)S(1)} %get-tuple-element.68), channel_id=1, source_target_pairs={{1,0},{3,2},{5,4},{7,6},{9,8},{11,10},{13,12},{15,14},{17,16},{19,... | collective-permute-start | bytes 589832 | tf_op jit(solution)/shard_map/ppermute | solution.py:23
  128.3 2.0 copy-start.15
  132.7 16.5 %copy-start.7 = (bf16[2,256,256]{1,2,0:T(8,128)(2,1)S(1)}, bf16[2,256,256]{1,2,0:T(8,128)(2,1)}, u32[]{:S(2)}) copy-start(bf16[2,256,256]{1,2,0:T(8,128)(2,1)} %get-tuple-element.34) | copy-start | bytes 786436
  132.7 17.4 %copy-start.14 = (s32[8,16]{1,0:T(8,128)S(1)}, s32[8,16]{1,0:T(8,128)}, u32[]{:S(2)}) copy-start(s32[8,16]{1,0:T(8,128)} %param.10) | copy-start | bytes 1540
  134.8 68.8 %all-to-all-start = ((bf16[1,2,512,512]{3,1,0,2:T(2,128)(2,1)}), bf16[1,2,512,512]{3,1,0,2:T(2,128)(2,1)S(1)}, u32[]{:S(2)}, u32[]{:S(2)}) async-start(bf16[1,2,512,512]{3,1,0,2:T(2,128)(2,1)} %copy.59), calls=%async_computation | async-start | bytes 2097152 | tf_op jit(solution)/shard_map/all_to_all | solution.py:150
  149.2 52.0 %all-reduce.4.cloned.1.call-start = ((), (), s32[]{:S(2)}) async-start(), calls=%async_computation.1 | async-start | bytes 1048576 | tf_op jit(solution)/shard_map/psum | solution.py:140
Sparse Core Ops, SparseCore 0:
  152.9 48.2 all-reduce.3
where the time goes:
time: 223 us; the launch traced here: 222 us
  waiting for transfers between devices  72.1 us (32%)
  local copies, waits for them, and re-layouts  42.3 us (19%)
  other arithmetic  41.9 us (19%)
  starting transfers between devices  35.1 us (16%)
  matrix products  16 us (7%)
  between operations  14.4 us (6%)
    psum x1, waiting for transfers between devices, body(): lax.psum(probe_part.astype(jnp.bfloat16), ('sy', 'sx')).astype(jnp.float32)  50.9 us
    scatter x10, local copies, waits for them, and re-layouts  18.8 us
    ppermute x4, starting transfers between devices, with_halo(): lax.ppermute(tail, axis, [(i, (i + 1) % count) for i in range(ends)])  15.3 us
    ppermute x4, waiting for transfers between devices, with_halo(): lax.ppermute(head, axis, [((i + 1) % count, i) for i in range(ends)])  15.3 us
    scatter x4, other arithmetic  14.4 us
    all_to_all x1, starting transfers between devices, body(): lax.all_to_all(sinogram, ('ang', 'sx'), split_axis=2, concat_axis=0, tile...  14.4 us
    dot_general x2, matrix products, right_product(): jnp.einsum('btrc,tcsq->bsrq', fields, matrix, preferred_element_type=jnp....  8.42 us
    ppermute x4, waiting for transfers between devices, with_halo(): lax.ppermute(tail, axis, [(i, (i + 1) % count) for i in range(ends)])  5.81 us
  transfers between devices with their start and end apart: 10, of which 7 were waited for; matrix products, arithmetic and copies ran while one was open for 7% of the time, Pallas kernels for 0%

commit v1 on v0

--- a/solution.py
+++ b/solution.py
@@ -8,6 +8,11 @@
 PATCH = 256
 RIM = 64
 BLK = 128
+
+
+def by_each_axis(value, first, second):
+    partial_2 = lax.psum(value, first)
+    return lax.psum(partial_2, second)
 
 
 def with_halo(cells, sides, width):
@@ -137,7 +142,7 @@
     )
     object_grad = fold_rims(fold_rims(returned, 1, tile_rows), 2, tile_cols)
     tile_count = lax.axis_size("sy") * lax.axis_size("sx")
-    probe_total = lax.psum(probe_part.astype(jnp.bfloat16), ("sy", "sx")).astype(jnp.float32)
+    probe_total = by_each_axis(probe_part.astype(jnp.bfloat16), "sx", "sy").astype(jnp.float32)
     probe_grad = (probe_total / math.sqrt(starts.shape[0] * tile_count))[None]
     line_blocks = block_values.shape[0]
     width_all = line_blocks * block_values.shape[2]

time: 223 us -> 263 us (1.18)
  waiting for transfers between devices: 72.1 us -> 111 us
    psum x1 -> x2, waiting for transfers between devices: 50.9 us -> 90.1 us  [the longest x1 45.4 us: by_each_axis(): return lax.psum(partial_2, second)]
  transfers between devices with their start and end apart: 10 -> 11, of which waited for: 7 -> 8; matrix products, arithmetic and copies ran while one was open for 7% -> 6% of each run, Pallas kernels for 0% -> 0%
where the time goes in v1:
time: 263 us; the launch traced here: 261 us
  waiting for transfers between devices  111 us (42%)
  local copies, waits for them, and re-layouts  42.3 us (16%)
  other arithmetic  41.9 us (16%)
  starting transfers between devices  35.2 us (13%)
  matrix products  16 us (6%)
  between operations  14.4 us (5%)
    psum x1, waiting for transfers between devices, by_each_axis(): return lax.psum(partial_2, second)  45.4 us
    psum x1, waiting for transfers between devices, by_each_axis(): partial_2 = lax.psum(value, first)  44.7 us
    scatter x10, local copies, waits for them, and re-layouts  18.8 us
    ppermute x4, starting transfers between devices, with_halo(): lax.ppermute(tail, axis, [(i, (i + 1) % count) for i in range(ends)])  15.3 us
    ppermute x4, waiting for transfers between devices, with_halo(): lax.ppermute(head, axis, [((i + 1) % count, i) for i in range(ends)])  15.3 us
    scatter x4, other arithmetic  14.4 us
    all_to_all x1, starting transfers between devices, body(): lax.all_to_all(sinogram, ('ang', 'sx'), split_axis=2, concat_axis=0, tile...  14.4 us
    dot_general x2, matrix products, right_product(): jnp.einsum('btrc,tcsq->bsrq', fields, matrix, preferred_element_type=jnp....  8.42 us
  transfers between devices with their start and end apart: 11, of which 8 were waited for; matrix products, arithmetic and copies ran while one was open for 6% of the time, Pallas kernels for 0%

profile of v1, /device:TPU:2, one launch (start us, length us, event | category | flops | bytes accessed | tf_op | source)
XLA Modules:
  0.0 261.0 jit_solution(15523240690853105973)
XLA Ops:
  7.2 1.1 fusion.79
  8.3 5.1 %collective-permute-start = (bf16[2,64,512]{2,1,0:T(8,128)(2,1)S(1)}, bf16[2,64,512]{2,1,0:T(8,128)(2,1)S(1)}, u32[]{:S(2)}, u32[]{:S(2)}) collective-permute-start(bf16[2,64,512]{2,1,0:T(8,128)(2,1)S(1)} %get-tuple-element.75), channel_id=1, source_target_pairs={{0,2},{1,3},{4,6},{5,7},{8,10},{9,11},{12,14},{13,15},{16,18},{17,... | collective-permute-start | bytes 393224 | tf_op jit(solution)/shard_map/ppermute | solution.py:26
  13.4 1.3 collective-permute-start.1
  14.7 1.0 fusion.55
  15.7 1.0 multiply_convert_fusion
  16.7 1.0 negate_convert_fusion
  17.6 0.8 compare_select_fusion.3
  18.5 1.3 slice_bitcast_fusion.3
  19.8 0.7 broadcast_clamp_fusion
  20.5 0.8 fusion.47
  21.3 0.4 collective-permute-done.1
  22.0 1.0 pad_maximum_fusion.8
  23.0 3.3 %collective-permute-start.2 = (bf16[2,640,64]{2,1,0:T(8,128)(2,1)}, bf16[2,640,64]{2,1,0:T(8,128)(2,1)}, u32[]{:S(2)}, u32[]{:S(2)}) collective-permute-start(bf16[2,640,64]{2,1,0:T(8,128)(2,1)} %get-tuple-element.71), channel_id=1, source_target_pairs={{0,1},{2,3},{4,5},{6,7},{8,9},{10,11},{12,13},{14,15},{16,17},{18,... | collective-permute-start | bytes 491528 | tf_op jit(solution)/shard_map/ppermute | solution.py:26
  26.3 1.5 collective-permute-start.3
  28.0 1.0 copy.50
  29.0 1.8 copy.54
  30.8 2.0 maximum_bitcast_fusion.3
  32.9 4.5 %collective-permute-done.3 = bf16[2,640,64]{2,1,0:T(8,128)(2,1)} collective-permute-done((bf16[2,640,64]{2,1,0:T(8,128)(2,1)}, bf16[2,640,64]{2,1,0:T(8,128)(2,1)}, u32[]{:S(2)}, u32[]{:S(2)}) %collective-permute-start.3) | collective-permute-done | bytes 163872 | tf_op jit(solution)/shard_map/ppermute | solution.py:28
  37.4 2.2 pad_maximum_fusion
  39.6 5.8 %while.2 = (s32[]{:T(128)}, bf16[2,640,640]{2,1,0:T(8,128)(2,1)S(1)}, s32[2,3]{1,0:T(2,128)S(1)}, bf16[2,2,256,256]{3,2,1,0:T(8,128)(2,1)}, s32[]{:T(128)}) while((s32[]{:T(128)}, bf16[2,640,640]{2,1,0:T(8,128)(2,1)S(1)}, s32[2,3]{1,0:T(2,128)S(1)}, bf16[2,2,256,256]{3,2,1,0:T(8,128)(2,1)}, s32[]{:T(128)}) %tuple.63), condition=%wide.while_cond, body=%wide.while_body.sunk | while | flops 2 | bytes 525929 | solution.py:73
  39.6 0.7 fusion.86
  40.2 2.2 bitcast_dynamic-update-slice_fusion.2
  42.5 0.7 fusion.86
  43.1 2.2 bitcast_dynamic-update-slice_fusion.2
  45.4 1.2 bitcast_convert_fusion.4
  47.0 1.3 subtract_convert_fusion
  48.3 5.0 %fusion.15 = (f32[4,256,256]{1,2,0:T(8,128)}, f32[2,256,4,256,1]{3,1,4,2,0:T(8,128)}) fusion(bf16[4,1,256,256]{2,3,1,0:T(8,128)(2,1)} %bitcast.227, bf16[4,1,256,256]{2,3,1,0:T(8,128)(2,1)} %bitcast.226, bf16[1,256,2,256]{3,1,2,0:T(8,128)(2,1)S(1)} %copy-done.10, bf16[1,256,2,256]{3,1,2,0:T(8,128)(2,1)S(1)} %copy-done.9, ...), kind=kOutput, calls=%fused_computation.31 | convolution fusion | flops 1078198272 | bytes 5242880 | tf_op jit(solution)/shard_map/btrc,tcsq->bsrq/dot_general | solution.py:69
  53.3 1.4 bitcast_reduce_fusion
  54.7 1.1 mul.359
  55.8 3.4 %fusion.33 = f32[2,256,4,256,1]{3,1,4,2,0:T(8,128)S(1)} fusion(bf16[2,256,2,256,1]{3,1,2,0,4:T(8,128)(2,1)} %get-tuple-element.89, bf16[1,256,2,256]{3,1,2,0:T(8,128)(2,1)S(1)} %get-tuple-element.80, bf16[1,256,2,256]{3,1,2,0:T(8,128)(2,1)} %copy-done.5, f32[2,256,4,256,1]{3,1,4,2,0:T(8,128)} %get-tuple-element.88, f32[4,256,256]{1,2,0:T(8,128)} %bitcast.218), kind=kOutput, calls=%fused_computation.49 | convolution fusion | flops 1076363264 | bytes 6291456 | tf_op jit(solution)/shard_map/btrc,tcsq->bsrq/dot_general | solution.py:69
  59.2 2.7 %add_reduce_fusion = (bf16[2,256,256]{1,2,0:T(8,128)(2,1)S(1)}, bf16[2,256,256]{1,2,0:T(8,128)(2,1)}, f32[2,256,256]{1,2,0:T(8,128)S(1)}, f32[2,256,256]{1,2,0:T(8,128)S(1)}) fusion(f32[2,2,2,256,256]{3,4,1,0,2:T(8,128)S(1)} %bitcast.212, f32[2,256,256]{1,2,0:T(8,128)} %copy-done.4, f32[2,256,256]{1,2,0:T(8,128)} %copy-done.3, ...), kind=kLoop, calls=%fused_computation.64 | loop fusion | flops 3670016 | bytes 5767168 | tf_op jit(solution)/shard_map/reduce_sum | solution.py:109
  62.0 3.1 %broadcast_in_dim.40 = f32[2,2,640,640]{3,2,1,0:T(8,128)} broadcast(f32[]{:T(128)} %constant.70.clone.1), dimensions={} | broadcast | bytes 6553604 | tf_op jit(solution)/shard_map/vmap(vmap())/broadcast_in_dim;vmap()/broadcast_in_dim | solution.py:137
  65.1 33.3 %while.3 = (s32[]{:T(128)}, f32[2,2,640,640]{3,2,1,0:T(8,128)}, s32[2,4]{1,0:T(2,128)S(1)}, f32[2,2,256,256]{2,3,0,1:T(8,128)S(1)}, s32[]{:T(128)}, /*index=5*/s32[4]{0:T(128)S(1)}, s32[]{:T(128)}) while((s32[]{:T(128)}, f32[2,2,640,640]{3,2,1,0:T(8,128)}, s32[2,4]{1,0:T(2,128)S(1)}, f32[2,2,256,256]{2,3,0,1:T(8,128)S(1)}, s32[]{:T(128)}, ...), condition=%wide.while_cond.1, body=%wide.while_body.1.sunk | while | flops 131101 | bytes 4718791 | solution.py:137
  65.1 0.7 fusion.87
  65.8 3.3 %and_reduce_fusion.2 = pred[]{:T(512)} fusion(s32[4]{0:T(128)S(1)} %get-tuple-element.187, s32[1]{0:T(128)} %bitcast.208, s32[1]{0:T(128)} %bitcast.209, s32[1]{0:T(128)} %bitcast.210, s32[1]{0:T(128)} %bitcast.211), kind=kLoop, calls=%fused_computation.4.clone.1 | loop fusion | flops 27 | bytes 33 | tf_op jit(solution)/shard_map/vmap(vmap())/scatter
  69.3 3.9 %dynamic-slice_select_fusion.2 = f32[1,2,256,256]{3,2,1,0:T(8,128)S(1)} fusion(f32[1,2,256,256]{3,2,1,0:T(8,128)S(1)} %copy.105, f32[2,2,640,640]{3,2,1,0:T(8,128)} %get-tuple-element.176, s32[]{:T(128)} %bitcast.205, s32[]{:T(128)} %bitcast.206, s32[]{:T(128)} %bitcast.207, pred[]{:T(512)} %and_reduce_fusion.2), kind=kLoop, calls=%fused_computation.3.clone.1 | loop fusion | flops 131072 | bytes 1572877 | tf_op jit(solution)/shard_map/vmap(vmap())/scatter
  73.3 8.4 %dynamic-update-slice.8 = f32[2,2,640,640]{3,2,1,0:T(8,128)} dynamic-update-slice(f32[2,2,640,640]{3,2,1,0:T(8,128)} %get-tuple-element.176, f32[1,2,256,256]{3,2,1,0:T(8,128)S(1)} %dynamic-slice_select_fusion.2, s32[]{:T(128)} %bitcast.205, s32[]{:T(128)} %constant.71.clone.1..sunk, s32[]{:T(128)} %bitcast.206, s32[]{:T(128)} %bitcast.207) | dynamic-update-slice | bytes 1048580 | tf_op jit(solution)/shard_map/vmap(vmap())/scatter
  81.7 0.7 fusion.87
  82.4 3.3 %and_reduce_fusion.2 = pred[]{:T(512)} fusion(s32[4]{0:T(128)S(1)} %get-tuple-element.187, s32[1]{0:T(128)} %bitcast.208, s32[1]{0:T(128)} %bitcast.209, s32[1]{0:T(128)} %bitcast.210, s32[1]{0:T(128)} %bitcast.211), kind=kLoop, calls=%fused_computation.4.clone.1 | loop fusion | flops 27 | bytes 33 | tf_op jit(solution)/shard_map/vmap(vmap())/scatter
  85.9 3.9 %dynamic-slice_select_fusion.2 = f32[1,2,256,256]{3,2,1,0:T(8,128)S(1)} fusion(f32[1,2,256,256]{3,2,1,0:T(8,128)S(1)} %copy.105, f32[2,2,640,640]{3,2,1,0:T(8,128)} %get-tuple-element.176, s32[]{:T(128)} %bitcast.205, s32[]{:T(128)} %bitcast.206, s32[]{:T(128)} %bitcast.207, pred[]{:T(512)} %and_reduce_fusion.2), kind=kLoop, calls=%fused_computation.3.clone.1 | loop fusion | flops 131072 | bytes 1572877 | tf_op jit(solution)/shard_map/vmap(vmap())/scatter
  89.8 8.6 %dynamic-update-slice.8 = f32[2,2,640,640]{3,2,1,0:T(8,128)} dynamic-update-slice(f32[2,2,640,640]{3,2,1,0:T(8,128)} %get-tuple-element.176, f32[1,2,256,256]{3,2,1,0:T(8,128)S(1)} %dynamic-slice_select_fusion.2, s32[]{:T(128)} %bitcast.205, s32[]{:T(128)} %constant.71.clone.1..sunk, s32[]{:T(128)} %bitcast.206, s32[]{:T(128)} %bitcast.207) | dynamic-update-slice | bytes 1048580 | tf_op jit(solution)/shard_map/vmap(vmap())/scatter
  98.4 3.8 %reduce_sum.66 = bf16[2,640,640]{2,1,0:T(8,128)(2,1)S(1)} reduce(f32[2,2,640,640]{3,2,1,0:T(8,128)} %get-tuple-element.16, f32[]{:T(128)} %constant.70.clone.1), dimensions={0}, to_apply=%region_5.6 | reduce | flops 819200 | bytes 8192004 | tf_op jit(solution)/shard_map/reduce_sum | solution.py:139
  102.2 5.6 %collective-permute-start.4 = (bf16[2,64,640]{2,1,0:T(8,128)(2,1)S(1)}, bf16[2,64,640]{2,1,0:T(8,128)(2,1)S(1)}, u32[]{:S(2)}, u32[]{:S(2)}) collective-permute-start(bf16[2,64,640]{2,1,0:T(8,128)(2,1)S(1)} %get-tuple-element.69), channel_id=1, source_target_pairs={{0,2},{1,3},{4,6},{5,7},{8,10},{9,11},{12,14},{13,15},{16,18},{17,... | collective-permute-start | bytes 491528 | tf_op jit(solution)/shard_map/ppermute | solution.py:26
  107.9 1.3 collective-permute-start.5
  109.2 1.5 collective-permute-done.4
  110.7 6.3 %collective-permute-done.5 = bf16[2,64,640]{2,1,0:T(8,128)(2,1)S(1)} collective-permute-done((bf16[2,64,640]{2,1,0:T(8,128)(2,1)S(1)}, bf16[2,64,640]{2,1,0:T(8,128)(2,1)S(1)}, u32[]{:S(2)}, u32[]{:S(2)}) %collective-permute-start.5) | collective-permute-done | bytes 163872 | tf_op jit(solution)/shard_map/ppermute | solution.py:28
  117.1 1.3 collective-permute-start.6
  118.5 1.3 collective-permute-start.7
  119.8 4.3 %collective-permute-done.6 = bf16[2,768,64]{2,1,0:T(8,128)(2,1)S(1)} collective-permute-done((bf16[2,768,64]{2,1,0:T(8,128)(2,1)S(1)}, bf16[2,768,64]{2,1,0:T(8,128)(2,1)S(1)}, u32[]{:S(2)}, u32[]{:S(2)}) %collective-permute-start.6) | collective-permute-done | bytes 196640 | tf_op jit(solution)/shard_map/ppermute | solution.py:26
  124.1 4.1 %collective-permute-done.7 = bf16[2,768,64]{2,1,0:T(8,128)(2,1)S(1)} collective-permute-done((bf16[2,768,64]{2,1,0:T(8,128)(2,1)S(1)}, bf16[2,768,64]{2,1,0:T(8,128)(2,1)S(1)}, u32[]{:S(2)}, u32[]{:S(2)}) %collective-permute-start.7) | collective-permute-done | bytes 196640 | tf_op jit(solution)/shard_map/ppermute | solution.py:28
  128.3 2.0 maximum_convert_fusion
  131.0 1.8 convert_bitcast_fusion
  132.7 2.1 copy.59
  134.8 14.4 %all-to-all-start = ((bf16[1,2,512,512]{3,1,0,2:T(2,128)(2,1)}), bf16[1,2,512,512]{3,1,0,2:T(2,128)(2,1)S(1)}, u32[]{:S(2)}, u32[]{:S(2)}) async-start(bf16[1,2,512,512]{3,1,0,2:T(2,128)(2,1)} %copy.59), calls=%async_computation | async-start | bytes 2097152 | tf_op jit(solution)/shard_map/all_to_all | solution.py:155
  149.3 0.8 pad_maximum_fusion.2
  150.2 44.7 %all-reduce.5.cloned.1.call-done = bf16[2,2,256,256]{2,3,0,1:T(8,128)(2,1)} async-done(((bf16[2,2,256,256]{2,3,0,1:T(8,128)(2,1)}), bf16[2,2,256,256]{2,3,0,1:T(8,128)(2,1)}) %all-reduce.5.cloned.1.call-update) | async-done | bytes 524304 | tf_op jit(solution)/shard_map/psum | solution.py:14
  195.1 45.4 %all-reduce.7.cloned.1.call-done = bf16[2,2,256,256]{2,3,0,1:T(8,128)(2,1)} async-done(((bf16[2,2,256,256]{2,3,0,1:T(8,128)(2,1)}), bf16[2,2,256,256]{2,3,0,1:T(8,128)(2,1)}) %all-reduce.7.cloned.1.call-update) | async-done | bytes 524304 | tf_op jit(solution)/shard_map/psum | solution.py:15
  240.4 1.1 multiply_bitcast_fusion
  241.6 1.3 copy.66
  243.3 4.6 %bitcast_convert_fusion = bf16[64,2,4,1024]{3,0,2,1:T(8,128)(2,1)S(1)} fusion(s32[2,512]{1,0:T(2,128)S(1)} %multiply_add_fusion, bf16[64,2,2,4,512]{4,3,2,1,0:T(4,128)(2,1)S(1)} %bitcast.222), kind=kOutput, calls=%fused_computation.33 | convolution fusion | flops 1097334784 | bytes 2101248 | tf_op jit(solution)/shard_map/ascrt,stv->acrv/dot_general | solution.py:157
  248.2 1.4 copy.62
  249.6 1.0 gather_fusion
  250.6 2.9 %fusion.30 = f32[4,2,8,128]{3,0,1,2:T(4,128)S(1)} fusion(bf16[8,16,2,4,128]{4,3,2,1,0:T(4,128)(2,1)S(1)} %bitcast.221, bf16[8,16,128,128]{3,2,1,0:T(8,128)(2,1)} %param.11), kind=kOutput, calls=%fused_computation.48 | convolution fusion | flops 33554432 | bytes 4489216 | tf_op jit(solution)/shard_map/bkcru,bkuv->rcbv/dot_general | solution.py:163
  253.5 0.6 reshape.313
  (67 shorter events, 3.4 us)
Async XLA Ops:
  7.2 14.8 %copy-start = (bf16[1,2,512,512]{3,2,1,0:T(8,128)(2,1)S(1)}, bf16[1,2,512,512]{3,2,1,0:T(8,128)(2,1)}, u32[]{:S(2)}) copy-start(bf16[1,2,512,512]{3,2,1,0:T(8,128)(2,1)} %param.6) | copy-start | bytes 3145732
  8.3 13.0 %collective-permute-start = (bf16[2,64,512]{2,1,0:T(8,128)(2,1)S(1)}, bf16[2,64,512]{2,1,0:T(8,128)(2,1)S(1)}, u32[]{:S(2)}, u32[]{:S(2)}) collective-permute-start(bf16[2,64,512]{2,1,0:T(8,128)(2,1)S(1)} %get-tuple-element.75), channel_id=1, source_target_pairs={{0,2},{1,3},{4,6},{5,7},{8,10},{9,11},{12,14},{13,15},{16,18},{17,... | collective-permute-start | bytes 393224 | tf_op jit(solution)/shard_map/ppermute | solution.py:26
  13.4 8.4 %collective-permute-start.1 = (bf16[2,64,512]{2,1,0:T(8,128)(2,1)S(1)}, bf16[2,64,512]{2,1,0:T(8,128)(2,1)S(1)}, u32[]{:S(2)}, u32[]{:S(2)}) collective-permute-start(bf16[2,64,512]{2,1,0:T(8,128)(2,1)S(1)} %get-tuple-element.76), channel_id=1, source_target_pairs={{2,0},{3,1},{6,4},{7,5},{10,8},{11,9},{14,12},{15,13},{18,16},{19,... | collective-permute-start | bytes 393224 | tf_op jit(solution)/shard_map/ppermute | solution.py:28
  21.3 11.6 %copy-start.5 = (bf16[1,256,2,256]{3,1,2,0:T(8,128)(2,1)}, bf16[1,256,2,256]{3,1,2,0:T(8,128)(2,1)S(1)}, u32[]{:S(2)}) copy-start(bf16[1,256,2,256]{3,1,2,0:T(8,128)(2,1)S(1)} %get-tuple-element.83) | copy-start | bytes 786436
  21.3 11.6 %copy-start.8 = (bf16[1,256,2,256]{3,1,2,0:T(8,128)(2,1)}, bf16[1,256,2,256]{3,1,2,0:T(8,128)(2,1)S(1)}, u32[]{:S(2)}) copy-start(bf16[1,256,2,256]{3,1,2,0:T(8,128)(2,1)S(1)} %get-tuple-element.79) | copy-start | bytes 786436
  21.3 0.7 copy-start.11
  22.0 1.0 copy-start.12
  23.0 9.9 %collective-permute-start.2 = (bf16[2,640,64]{2,1,0:T(8,128)(2,1)}, bf16[2,640,64]{2,1,0:T(8,128)(2,1)}, u32[]{:S(2)}, u32[]{:S(2)}) collective-permute-start(bf16[2,640,64]{2,1,0:T(8,128)(2,1)} %get-tuple-element.71), channel_id=1, source_target_pairs={{0,1},{2,3},{4,5},{6,7},{8,9},{10,11},{12,13},{14,15},{16,17},{18,... | collective-permute-start | bytes 491528 | tf_op jit(solution)/shard_map/ppermute | solution.py:26
  26.3 11.1 %collective-permute-start.3 = (bf16[2,640,64]{2,1,0:T(8,128)(2,1)}, bf16[2,640,64]{2,1,0:T(8,128)(2,1)}, u32[]{:S(2)}, u32[]{:S(2)}) collective-permute-start(bf16[2,640,64]{2,1,0:T(8,128)(2,1)} %get-tuple-element.72), channel_id=1, source_target_pairs={{1,0},{3,2},{5,4},{7,6},{9,8},{11,10},{13,12},{15,14},{17,16},{19,... | collective-permute-start | bytes 491528 | tf_op jit(solution)/shard_map/ppermute | solution.py:28
  39.5 7.4 %copy-start.1 = (f32[2,256,256]{1,2,0:T(8,128)S(1)}, f32[2,256,256]{1,2,0:T(8,128)}, u32[]{:S(2)}) copy-start(f32[2,256,256]{1,2,0:T(8,128)} %copy.50) | copy-start | bytes 1572868
  45.4 2.9 %copy-start.9 = (bf16[1,256,2,256]{3,1,2,0:T(8,128)(2,1)S(1)}, bf16[1,256,2,256]{3,1,2,0:T(8,128)(2,1)}, u32[]{:S(2)}) copy-start(bf16[1,256,2,256]{3,1,2,0:T(8,128)(2,1)} %copy-done.8) | copy-start | bytes 786436
  45.4 2.9 %copy-start.10 = (bf16[1,256,2,256]{3,1,2,0:T(8,128)(2,1)S(1)}, bf16[1,256,2,256]{3,1,2,0:T(8,128)(2,1)}, u32[]{:S(2)}) copy-start(bf16[1,256,2,256]{3,1,2,0:T(8,128)(2,1)} %get-tuple-element.84) | copy-start | bytes 786436
  46.8 6.5 %copy-start.3 = (f32[2,256,256]{1,2,0:T(8,128)}, f32[2,256,256]{1,2,0:T(8,128)S(1)}, u32[]{:S(2)}) copy-start(f32[2,256,256]{1,2,0:T(8,128)S(1)} %copy.49) | copy-start | bytes 1572868
  47.0 6.3 %copy-start.4 = (f32[2,256,256]{1,2,0:T(8,128)}, f32[2,256,256]{1,2,0:T(8,128)S(1)}, u32[]{:S(2)}) copy-start(f32[2,256,256]{1,2,0:T(8,128)S(1)} %copy.51) | copy-start | bytes 1572868
  48.3 6.4 %copy-start.6 = (bf16[1,1,1,2,256,256]{4,5,3,2,1,0:T(8,128)(2,1)S(1)}, bf16[1,1,1,2,256,256]{4,5,3,2,1,0:T(8,128)(2,1)}, u32[]{:S(2)}) copy-start(bf16[1,1,1,2,256,256]{4,5,3,2,1,0:T(8,128)(2,1)} %copy.54) | copy-start | bytes 786436
  55.8 3.4 %copy-start.2 = (f32[2,256,256]{1,2,0:T(8,128)S(1)}, f32[2,256,256]{1,2,0:T(8,128)}, u32[]{:S(2)}) copy-start(f32[2,256,256]{1,2,0:T(8,128)} %copy.50) | copy-start | bytes 1572868
  62.0 3.2 %copy-start.13 = (s32[4]{0:T(128)S(1)}, s32[4]{0:T(128)}, u32[]{:S(2)}) copy-start(s32[4]{0:T(128)} %constant.300) | copy-start | bytes 52
  102.2 8.4 %collective-permute-start.4 = (bf16[2,64,640]{2,1,0:T(8,128)(2,1)S(1)}, bf16[2,64,640]{2,1,0:T(8,128)(2,1)S(1)}, u32[]{:S(2)}, u32[]{:S(2)}) collective-permute-start(bf16[2,64,640]{2,1,0:T(8,128)(2,1)S(1)} %get-tuple-element.69), channel_id=1, source_target_pairs={{0,2},{1,3},{4,6},{5,7},{8,10},{9,11},{12,14},{13,15},{16,18},{17,... | collective-permute-start | bytes 491528 | tf_op jit(solution)/shard_map/ppermute | solution.py:26
  107.9 9.1 %collective-permute-start.5 = (bf16[2,64,640]{2,1,0:T(8,128)(2,1)S(1)}, bf16[2,64,640]{2,1,0:T(8,128)(2,1)S(1)}, u32[]{:S(2)}, u32[]{:S(2)}) collective-permute-start(bf16[2,64,640]{2,1,0:T(8,128)(2,1)S(1)} %get-tuple-element.70), channel_id=1, source_target_pairs={{2,0},{3,1},{6,4},{7,5},{10,8},{11,9},{14,12},{15,13},{18,16},{19,... | collective-permute-start | bytes 491528 | tf_op jit(solution)/shard_map/ppermute | solution.py:28
  117.1 6.9 %collective-permute-start.6 = (bf16[2,768,64]{2,1,0:T(8,128)(2,1)S(1)}, bf16[2,768,64]{2,1,0:T(8,128)(2,1)S(1)}, u32[]{:S(2)}, u32[]{:S(2)}) collective-permute-start(bf16[2,768,64]{2,1,0:T(8,128)(2,1)S(1)} %get-tuple-element.67), channel_id=1, source_target_pairs={{0,1},{2,3},{4,5},{6,7},{8,9},{10,11},{12,13},{14,15},{16,17},{18,... | collective-permute-start | bytes 589832 | tf_op jit(solution)/shard_map/ppermute | solution.py:26
  118.5 9.7 %collective-permute-start.7 = (bf16[2,768,64]{2,1,0:T(8,128)(2,1)S(1)}, bf16[2,768,64]{2,1,0:T(8,128)(2,1)S(1)}, u32[]{:S(2)}, u32[]{:S(2)}) collective-permute-start(bf16[2,768,64]{2,1,0:T(8,128)(2,1)S(1)} %get-tuple-element.68), channel_id=1, source_target_pairs={{1,0},{3,2},{5,4},{7,6},{9,8},{11,10},{13,12},{15,14},{17,16},{19,... | collective-permute-start | bytes 589832 | tf_op jit(solution)/shard_map/ppermute | solution.py:28
  128.3 2.0 copy-start.15
  132.7 16.5 %copy-start.7 = (bf16[2,256,256]{1,2,0:T(8,128)(2,1)S(1)}, bf16[2,256,256]{1,2,0:T(8,128)(2,1)}, u32[]{:S(2)}) copy-start(bf16[2,256,256]{1,2,0:T(8,128)(2,1)} %get-tuple-element.34) | copy-start | bytes 786436
  132.7 62.2 %copy-start.14 = (s32[8,16]{1,0:T(8,128)S(1)}, s32[8,16]{1,0:T(8,128)}, u32[]{:S(2)}) copy-start(s32[8,16]{1,0:T(8,128)} %param.10) | copy-start | bytes 1540
  134.8 108.1 %all-to-all-start = ((bf16[1,2,512,512]{3,1,0,2:T(2,128)(2,1)}), bf16[1,2,512,512]{3,1,0,2:T(2,128)(2,1)S(1)}, u32[]{:S(2)}, u32[]{:S(2)}) async-start(bf16[1,2,512,512]{3,1,0,2:T(2,128)(2,1)} %copy.59), calls=%async_computation | async-start | bytes 2097152 | tf_op jit(solution)/shard_map/all_to_all | solution.py:155
  149.2 45.7 %all-reduce.5.cloned.1.call-start = ((), (), s32[]{:S(2)}) async-start(), calls=%async_computation.1 | async-start | bytes 1048576 | tf_op jit(solution)/shard_map/psum | solution.py:14
  150.1 90.3 %all-reduce.7.cloned.1.call-start = ((), (), s32[]{:S(2)}) async-start(), calls=%async_computation.2 | async-start | bytes 1048576 | tf_op jit(solution)/shard_map/psum | solution.py:15
Sparse Core Ops, SparseCore 0:
  153.2 41.6 all-reduce.4
  197.5 42.8 all-reduce.6
